TPU v7x, 32 devices: a whole 2x2x4 slice. The times are simulated.
32 devices in a mesh: space: 4 (over y, x), vel: 8 (over z, core).
Axes of the slice: x: 2, y: 2, z: 4, core: 2. Of those that a mesh axis runs over, the one named last changes fastest.
Arguments:
- cotangent: float32 [8192, 128, 128], P('vel', 'space'), may hold values from -6 to 6
- speed: float32 [3, 8192], P(None, 'vel'), may hold values from 0.1 to 3
- direction: int32 [3, 8192], P(None, 'vel'), may hold values from 0 to 1
- macroscopic_record: float32 [3, 5, 128, 128], P(None, None, 'space'), may hold values from -1 to 2, as said below
Outputs:
- gradient: float32 [8192, 128, 128], P('vel', 'space')
Inputs may be any that keep to these rules, and one draw needn't show every extreme that they name: `direction`: 1 marks a positive velocity component, 0 a negative one. `macroscopic_record`: density and temperature lie between 0.5 and 2, flow velocity components between -1 and 1.
All inputs are finite; a program needn't handle non-finite values.
Results may differ from a plain program's by a relative error of at most 0.00013.
Values sent between devices are 32-bit elements; how exact they have to be, the bound alone decides.
No kernel may reach another device: no remote copies, remote signals or barrier semaphores. Data moves between devices by JAX's collectives and lax.ppermute only.
A program may use at most 128 MiB of HBM per device.

v0:
```python
import math
import jax
import jax.numpy as jnp
from jax import lax
from jax.sharding import PartitionSpec as P

SPEED_POINTS = 8192
STEPS = 3
courant_number = 0.1
region_capacity = 216.0
mode_gains = (
    1.0,
    1.0,
    1.0,
    1.0,
    1.0,
    -0.5,
    -0.5,
    -0.5,
    -0.5,
    -0.5,
    1.0 / 3.0,
    1.0 / 3.0,
    1.0 / 3.0,
)
monomials = [
    (first, second, degree - first - second)
    for degree in range(4)
    for first in range(degree, -1, -1)
    for second in range(degree - first, -1, -1)
]
monomial_place = {exponents: place for place, exponents in enumerate(monomials)}


def with_halo(x, sides, width):
    for axis, dim in sides:
        peers, length = (lax.axis_size(axis), x.shape[dim])
        up = [(i, (i + 1) % peers) for i in range(peers)]
        down = [(j, i) for i, j in up]
        last = lax.slice_in_dim(x, length - width, length, axis=dim)
        first = lax.slice_in_dim(x, 0, width, axis=dim)
        before = lax.ppermute(last, axis, up)
        after = lax.ppermute(first, axis, down)
        x = jnp.concatenate([before, x, after], axis=dim)
    return x


def raise_to(values, exponent):
    result = jnp.ones_like(values)
    for repeat in range(exponent):
        result = result * values
    return result


def poly_mul(left, right):
    result = {}
    for left_key, left_coef in left.items():
        for right_key, right_coef in right.items():
            joined = (
                left_key[0] + right_key[0],
                left_key[1] + right_key[1],
                left_key[2] + right_key[2],
            )
            product = left_coef * right_coef
            result[joined] = result[joined] + product if joined in result else product
    return result


def poly_comb(terms):
    result = {}
    for weight, poly in terms:
        for poly_key, poly_coef in poly.items():
            scaled = weight * poly_coef
            result[poly_key] = result[poly_key] + scaled if poly_key in result else scaled
    return result


def hermite_polys(flow_rows, reciprocal_factor):
    linear = []
    for component in range(3):
        unit_key = tuple((1 if other == component else 0 for other in range(3)))
        linear.append(
            {unit_key: reciprocal_factor, (0, 0, 0): -flow_rows[component] * reciprocal_factor}
        )
    comp_x, comp_y, comp_z = linear
    unit_poly = {(0, 0, 0): 1.0}
    square_x = poly_mul(comp_x, comp_x)
    square_y = poly_mul(comp_y, comp_y)
    square_z = poly_mul(comp_z, comp_z)
    square = poly_comb([(1.0, square_x), (1.0, square_y), (1.0, square_z)])
    shifted = poly_comb([(1.0, square), (-5.0, unit_poly)])
    heat_scale = 1.0 / math.sqrt(10.0)
    return [
        unit_poly,
        comp_x,
        comp_y,
        comp_z,
        poly_comb([(1.0 / math.sqrt(6.0), square), (-3.0 / math.sqrt(6.0), unit_poly)]),
        poly_mul(comp_x, comp_y),
        poly_mul(comp_x, comp_z),
        poly_mul(comp_y, comp_z),
        poly_comb([(0.5, square_x), (-0.5, square_y)]),
        poly_comb(
            [
                (1.0 / math.sqrt(12.0), square_x),
                (1.0 / math.sqrt(12.0), square_y),
                (-2.0 / math.sqrt(12.0), square_z),
            ]
        ),
        poly_comb([(heat_scale, poly_mul(comp_x, shifted))]),
        poly_comb([(heat_scale, poly_mul(comp_y, shifted))]),
        poly_comb([(heat_scale, poly_mul(comp_z, shifted))]),
    ]


def to_modes(raw_rows, polys, zeros_like):
    mode_rows = []
    for poly in polys:
        running = zeros_like
        for poly_key, poly_coef in poly.items():
            running = running + poly_coef * raw_rows[monomial_place[poly_key]]
        mode_rows.append(running)
    return mode_rows


def to_coeffs(mode_rows, polys, zeros_like):
    coeff_rows = [zeros_like for exponents in monomials]
    for mode_index, poly in enumerate(polys):
        scaled_mode = mode_gains[mode_index] * mode_rows[mode_index]
        for poly_key, poly_coef in poly.items():
            place = monomial_place[poly_key]
            coeff_rows[place] = coeff_rows[place] + poly_coef * scaled_mode
    return jnp.stack(coeff_rows)


def pad_both(values, along):
    extent = values.shape[along]
    lower_rim = lax.slice_in_dim(values, extent - 2, extent, axis=along)
    upper_rim = lax.slice_in_dim(values, 0, 2, axis=along)
    return jnp.concatenate([lower_rim, values, upper_rim], axis=along)


def upwind_back(padded, length, along, lam_col, positive):

    def window(start_at):
        return lax.slice_in_dim(padded, start_at, start_at + length, axis=along)

    center = window(2)
    nearer = jnp.where(positive, window(3), window(1))
    farther = jnp.where(positive, window(4), window(0))
    return center - 0.5 * lam_col * (3.0 * center - 4.0 * nearer + farther)


def shards(cotangent, speed, direction, macroscopic_record):
    rows_x = cotangent.shape[1]
    cols_y = cotangent.shape[2]
    velocity = (2 * direction - 1).astype(jnp.float32) * speed
    factors = courant_number * speed
    positive = direction > 0
    lam_x = factors[0][:, None, None]
    lam_y = factors[1][:, None, None]
    pos_x = positive[0][:, None, None]
    pos_y = positive[1][:, None, None]
    table = jnp.stack(
        [
            raise_to(velocity[0], exponents[0])
            * raise_to(velocity[1], exponents[1])
            * raise_to(velocity[2], exponents[2])
            for exponents in monomials
        ]
    )
    adjoint = cotangent
    for iteration_counter in range(STEPS - 1, -1, -1):
        moved_y = upwind_back(pad_both(adjoint, 2), cols_y, 2, lam_y, pos_y)
        padded_x = with_halo(moved_y, (("space", 1),), 2)
        advected = upwind_back(padded_x, rows_x, 1, lam_x, pos_x)
        particle_concentration = macroscopic_record[iteration_counter, 0]
        flow_rows = [macroscopic_record[iteration_counter, 1 + component] for component in range(3)]
        thermal_energy_level = macroscopic_record[iteration_counter, 4]
        reciprocal_factor = 1.0 / jnp.sqrt(thermal_energy_level)
        normalising_coefficient = (
            particle_concentration
            * (2.0 * math.pi * thermal_energy_level) ** (-1.5)
            * region_capacity
            / SPEED_POINTS
        )
        relaxation_rate = 0.3 * particle_concentration * jnp.sqrt(thermal_energy_level)
        peculiar = [
            (velocity[component][:, None, None] - flow_rows[component]) * reciprocal_factor
            for component in range(3)
        ]
        weight = normalising_coefficient * jnp.exp(
            -0.5 * (peculiar[0] ** 2 + peculiar[1] ** 2 + peculiar[2] ** 2)
        )
        raw_moments = jnp.einsum(
            "av,vxy->axy", table, weight * advected, precision=lax.Precision.HIGHEST
        )
        zero_cells = jnp.zeros_like(particle_concentration)
        summed = lax.psum(raw_moments, "vel")
        polys = hermite_polys(flow_rows, reciprocal_factor)
        coeffs = to_coeffs(to_modes(summed, polys, zero_cells), polys, zero_cells)
        returned = jnp.einsum("av,axy->vxy", table, coeffs, precision=lax.Precision.HIGHEST)
        adjoint = (1.0 - relaxation_rate) * advected + relaxation_rate * returned
    return adjoint


def solution(mesh):
    in_specs = (
        P("vel", "space", None),
        P(None, "vel"),
        P(None, "vel"),
        P(None, None, "space", None),
    )
    out_specs = P("vel", "space", None)
    return jax.shard_map(shards, mesh=mesh, in_specs=in_specs, out_specs=out_specs, check_vma=False)
```

profile of v0, /device:TPU:0, one launch (start us, length us, event | category | flops | bytes accessed | tf_op | source)
XLA Modules:
  0.0 712.7 jit_solution(4509849928719995497)
XLA Ops:
  8.0 16.5 %copy.21 = f32[1024,32,128]{0,2,1:T(8,128)} copy(f32[1024,32,128]{2,1,0:T(8,128)} %param.4) | data formatting | bytes 33554432 | tf_op args[0]
  26.9 34.9 %fusion.46 = f32[1024,32,128]{0,2,1:T(8,128)} fusion(f32[1024,32,128]{0,2,1:T(8,128)} %copy.21, f32[1024,32,2]{0,2,1:T(2,128)S(1)} %get-tuple-element.47, f32[1024,32,2]{0,2,1:T(2,128)S(1)} %get-tuple-element.46, f32[1024]{0:T(1024)S(1)} %bitcast.1794, pred[1024]{0:T(1024)(128)(4,1)S(1)} %get-tuple-element.6), kind=kLoop, calls=%fused_computation.70 | loop fusion | flops 50331648 | bytes 34083840 | tf_op jit(solution)/shard_map/sub | solution.py:151
  71.3 21.0 %collective-permute-done = f32[1024,2,128]{0,2,1:T(8,128)S(1)} collective-permute-done((f32[1024,2,128]{0,2,1:T(8,128)}, f32[1024,2,128]{0,2,1:T(8,128)S(1)}, u32[]{:S(2)}, u32[]{:S(2)}) %collective-permute-start) | collective-permute-done | bytes 1048608 | tf_op jit(solution)/shard_map/ppermute | solution.py:43
  92.3 22.2 %collective-permute-done.1 = f32[1024,2,128]{0,2,1:T(8,128)S(1)} collective-permute-done((f32[1024,2,128]{0,2,1:T(8,128)S(1)}, f32[1024,2,128]{0,2,1:T(8,128)S(1)}, u32[]{:S(2)}, u32[]{:S(2)}) %collective-permute-start.1) | collective-permute-done | bytes 1048608 | tf_op jit(solution)/shard_map/ppermute | solution.py:42
  114.6 27.7 %fusion.38 = f32[1024,32,128]{0,2,1:T(8,128)S(1)} fusion(f32[1024,32,128]{0,2,1:T(8,128)} %fusion.46, f32[1024,2,128]{0,2,1:T(8,128)S(1)} %collective-permute-done.1, f32[1024,2,128]{0,2,1:T(8,128)S(1)} %collective-permute-done, f32[1024]{0:T(1024)S(1)} %bitcast.1791, pred[1024]{0:T(1024)(128)(4,1)S(1)} %get-tuple-element.5), kind=kLoop, calls=%fused_computation.62 | loop fusion | flops 50331648 | bytes 35656704 | tf_op jit(solution)/shard_map/sub | solution.py:151
  142.3 23.4 %fusion.86 = f32[20,32,128]{2,0,1:T(8,128)S(1)} fusion(f32[1024,32,128]{0,2,1:T(8,128)S(1)} %fusion.38, f32[32,128]{1,0:T(8,128)S(1)} %get-tuple-element.55, f32[1024]{0:T(1024)S(1)} %bitcast.1803, f32[32,128]{1,0:T(8,128)S(1)} %get-tuple-element.56, f32[1024]{0:T(1024)S(1)} %bitcast.1800, f32[32,128]{1,0:T(8,128)S(1)} %get-tuple-element.58, ...), kind=kOutput, calls=%fused_computation.125 | convolution fusion | flops 1065353216 | bytes 17281024 | tf_op jit(solution)/shard_map/av,vxy->axy/dot_general | solution.py:195
  167.0 55.6 %all-reduce.4.cloned.1.call-done = f32[20,32,128]{2,1,0:T(8,128)} async-done(((f32[20,32,128]{2,1,0:T(8,128)}), f32[20,32,128]{2,1,0:T(8,128)}) %all-reduce.4.cloned.1.call-update) | async-done | bytes 327696 | tf_op jit(solution)/shard_map/psum | solution.py:199
  229.0 17.5 %multiply_add_fusion.2 = f32[1024,32,128]{0,2,1:T(8,128)S(1)} fusion(f32[1024,32,128]{0,2,1:T(8,128)} %copy-done.2, f32[32,128]{1,0:T(8,128)S(1)} %get-tuple-element.64, f32[32,128]{1,0:T(8,128)S(1)} %get-tuple-element.63, f32[20,32,128]{2,1,0:T(8,128)S(1)} %constant_dynamic-update-slice_fusion, f32[20,1024]{1,0:T(8,128)S(1)} %stack.12), kind=kOutput, calls=%fused_computation.124 | convolution fusion | flops 1019215872 | bytes 33996800 | tf_op jit(solution)/shard_map/av,axy->vxy/dot_general | solution.py:202
  252.9 34.8 %fusion.30 = f32[1024,32,128]{0,2,1:T(8,128)} fusion(f32[1024,32,128]{0,2,1:T(8,128)} %copy-done.1, f32[1024,32,2]{0,2,1:T(2,128)S(1)} %get-tuple-element.43, f32[1024,32,2]{0,2,1:T(2,128)S(1)} %get-tuple-element.42, f32[1024]{0:T(1024)S(1)} %bitcast.1795, pred[1024]{0:T(1024)(128)(4,1)S(1)} %get-tuple-element.6), kind=kLoop, calls=%fused_computation.54 | loop fusion | flops 50331648 | bytes 34083840 | tf_op jit(solution)/shard_map/sub | solution.py:151
  292.0 23.4 %collective-permute-done.2 = f32[1024,2,128]{0,2,1:T(8,128)S(1)} collective-permute-done((f32[1024,2,128]{0,2,1:T(8,128)S(1)}, f32[1024,2,128]{0,2,1:T(8,128)S(1)}, u32[]{:S(2)}, u32[]{:S(2)}) %collective-permute-start.2) | collective-permute-done | bytes 1048608 | tf_op jit(solution)/shard_map/ppermute | solution.py:43
  315.4 20.5 %collective-permute-done.3 = f32[1024,2,128]{0,2,1:T(8,128)S(1)} collective-permute-done((f32[1024,2,128]{0,2,1:T(8,128)S(1)}, f32[1024,2,128]{0,2,1:T(8,128)S(1)}, u32[]{:S(2)}, u32[]{:S(2)}) %collective-permute-start.3) | collective-permute-done | bytes 1048608 | tf_op jit(solution)/shard_map/ppermute | solution.py:42
  335.9 27.7 %fusion.22 = f32[1024,32,128]{0,2,1:T(8,128)S(1)} fusion(f32[1024,32,128]{0,2,1:T(8,128)} %fusion.30, f32[1024,2,128]{0,2,1:T(8,128)S(1)} %collective-permute-done.3, f32[1024,2,128]{0,2,1:T(8,128)S(1)} %collective-permute-done.2, f32[1024]{0:T(1024)S(1)} %bitcast.1792, pred[1024]{0:T(1024)(128)(4,1)S(1)} %get-tuple-element.5), kind=kLoop, calls=%fused_computation.46 | loop fusion | flops 50331648 | bytes 35656704 | tf_op jit(solution)/shard_map/sub | solution.py:151
  363.7 23.4 %fusion.70 = f32[20,32,128]{2,0,1:T(8,128)S(1)} fusion(f32[1024,32,128]{0,2,1:T(8,128)S(1)} %fusion.22, f32[32,128]{1,0:T(8,128)S(1)} %copy-done.9, f32[32,128]{1,0:T(8,128)S(1)} %copy-done.10, f32[32,128]{1,0:T(8,128)S(1)} %copy-done.12, f32[32,128]{1,0:T(8,128)S(1)} %copy-done.11, f32[32,128]{1,0:T(8,128)S(1)} %copy-done.8, f32[1024]{0:T(1024)S(1)} %bitcast.1804, ...), kind=kOutput, calls=%fused_computation.108 | convolution fusion | flops 1065353216 | bytes 17281024 | tf_op jit(solution)/shard_map/av,vxy->axy/dot_general | solution.py:195
  388.1 54.6 %all-reduce.6.cloned.1.call-done = f32[20,32,128]{2,1,0:T(8,128)} async-done(((f32[20,32,128]{2,1,0:T(8,128)}), f32[20,32,128]{2,1,0:T(8,128)}) %all-reduce.6.cloned.1.call-update) | async-done | bytes 327696 | tf_op jit(solution)/shard_map/psum | solution.py:199
  449.1 17.5 %multiply_add_fusion.1 = f32[1024,32,128]{0,2,1:T(8,128)S(1)} fusion(f32[1024,32,128]{0,2,1:T(8,128)} %copy-done.4, f32[32,128]{1,0:T(8,128)S(1)} %get-tuple-element.66, f32[32,128]{1,0:T(8,128)S(1)} %get-tuple-element.65, f32[20,32,128]{2,1,0:T(8,128)S(1)} %constant_dynamic-update-slice_fusion.20, f32[20,1024]{1,0:T(8,128)S(1)} %stack.12), kind=kOutput, calls=%fused_computation.107 | convolution fusion | flops 1019215872 | bytes 33996800 | tf_op jit(solution)/shard_map/av,axy->vxy/dot_general | solution.py:202
  466.6 6.2 copy-done
  473.0 34.8 %fusion.14 = f32[1024,32,128]{0,2,1:T(8,128)} fusion(f32[1024,32,128]{0,2,1:T(8,128)} %copy-done, f32[1024,32,2]{0,2,1:T(2,128)S(1)} %get-tuple-element.39, f32[1024,32,2]{0,2,1:T(2,128)S(1)} %get-tuple-element.38, f32[1024]{0:T(1024)S(1)} %bitcast.1796, pred[1024]{0:T(1024)(128)(4,1)S(1)} %get-tuple-element.6), kind=kLoop, calls=%fused_computation.38 | loop fusion | flops 50331648 | bytes 34083840 | tf_op jit(solution)/shard_map/sub | solution.py:151
  512.2 23.4 %collective-permute-done.4 = f32[1024,2,128]{0,2,1:T(8,128)S(1)} collective-permute-done((f32[1024,2,128]{0,2,1:T(8,128)S(1)}, f32[1024,2,128]{0,2,1:T(8,128)S(1)}, u32[]{:S(2)}, u32[]{:S(2)}) %collective-permute-start.4) | collective-permute-done | bytes 1048608 | tf_op jit(solution)/shard_map/ppermute | solution.py:43
  535.6 20.5 %collective-permute-done.5 = f32[1024,2,128]{0,2,1:T(8,128)S(1)} collective-permute-done((f32[1024,2,128]{0,2,1:T(8,128)S(1)}, f32[1024,2,128]{0,2,1:T(8,128)S(1)}, u32[]{:S(2)}, u32[]{:S(2)}) %collective-permute-start.5) | collective-permute-done | bytes 1048608 | tf_op jit(solution)/shard_map/ppermute | solution.py:42
  556.1 27.7 %fusion.6 = f32[1024,32,128]{0,2,1:T(8,128)S(1)} fusion(f32[1024,32,128]{0,2,1:T(8,128)} %fusion.14, f32[1024,2,128]{0,2,1:T(8,128)S(1)} %collective-permute-done.5, f32[1024,2,128]{0,2,1:T(8,128)S(1)} %collective-permute-done.4, f32[1024]{0:T(1024)S(1)} %bitcast.1793, pred[1024]{0:T(1024)(128)(4,1)S(1)} %get-tuple-element.5), kind=kLoop, calls=%fused_computation.30 | loop fusion | flops 50331648 | bytes 35656704 | tf_op jit(solution)/shard_map/sub | solution.py:151
  583.8 23.4 %fusion.54 = f32[20,32,128]{2,0,1:T(8,128)S(1)} fusion(f32[1024,32,128]{0,2,1:T(8,128)S(1)} %fusion.6, f32[32,128]{1,0:T(8,128)S(1)} %copy-done.6, f32[32,128]{1,0:T(8,128)S(1)} %copy-done.7, f32[32,128]{1,0:T(8,128)S(1)} %get-tuple-element.60, f32[32,128]{1,0:T(8,128)S(1)} %get-tuple-element.51, f32[32,128]{1,0:T(8,128)S(1)} %get-tuple-element.48, ...), kind=kOutput, calls=%fused_computation.91 | convolution fusion | flops 1065353216 | bytes 17281024 | tf_op jit(solution)/shard_map/av,vxy->axy/dot_general | solution.py:195
  608.0 54.9 %all-reduce.8.cloned.1.call-done = f32[20,32,128]{2,1,0:T(8,128)} async-done(((f32[20,32,128]{2,1,0:T(8,128)}), f32[20,32,128]{2,1,0:T(8,128)}) %all-reduce.8.cloned.1.call-update) | async-done | bytes 327696 | tf_op jit(solution)/shard_map/psum | solution.py:199
  669.2 19.1 %multiply_add_fusion = f32[1024,32,128]{0,2,1:T(8,128)} fusion(f32[1024,32,128]{0,2,1:T(8,128)} %copy-done.3, f32[32,128]{1,0:T(8,128)S(1)} %get-tuple-element.15, f32[32,128]{1,0:T(8,128)S(1)} %get-tuple-element.14, f32[20,32,128]{2,1,0:T(8,128)S(1)} %constant_dynamic-update-slice_fusion.40, f32[20,1024]{1,0:T(8,128)S(1)} %stack.12), kind=kOutput, calls=%fused_computation.90 | convolution fusion | flops 1019215872 | bytes 33996800 | tf_op jit(solution)/shard_map/av,axy->vxy/dot_general | solution.py:202
  688.3 17.4 %copy.32 = f32[1024,32,128]{2,1,0:T(8,128)} copy(f32[1024,32,128]{0,2,1:T(8,128)} %multiply_add_fusion) | data formatting | bytes 33554432 | tf_op jit(solution)/shard_map/add | solution.py:203
  (121 shorter events, 50.6 us)
Async XLA Ops:
  6.5 216.1 %all-reduce.4.cloned.1.call-start = ((), (), s32[]{:S(2)}) async-start(), calls=%async_computation | async-start | bytes 655360 | tf_op jit(solution)/shard_map/psum | solution.py:199
  26.9 43.7 %copy-start.5 = (f32[3,5,32,128]{3,2,1,0:T(8,128)S(1)}, f32[3,5,32,128]{3,2,1,0:T(8,128)}, u32[]{:S(2)}) copy-start(f32[3,5,32,128]{3,2,1,0:T(8,128)} %param.7) | copy-start | bytes 737284
  64.6 27.8 %collective-permute-start = (f32[1024,2,128]{0,2,1:T(8,128)}, f32[1024,2,128]{0,2,1:T(8,128)S(1)}, u32[]{:S(2)}, u32[]{:S(2)}) collective-permute-start(f32[1024,2,128]{0,2,1:T(8,128)} %get-tuple-element.44), channel_id=1, source_target_pairs={{8,0},{16,8},{24,16},{0,24},{9,1},{17,9},{25,17},{1,25},{10,2},{18... | collective-permute-start | bytes 3145736 | tf_op jit(solution)/shard_map/ppermute | solution.py:43
  68.5 46.1 %collective-permute-start.1 = (f32[1024,2,128]{0,2,1:T(8,128)S(1)}, f32[1024,2,128]{0,2,1:T(8,128)S(1)}, u32[]{:S(2)}, u32[]{:S(2)}) collective-permute-start(f32[1024,2,128]{0,2,1:T(8,128)S(1)} %get-tuple-element.45), channel_id=1, source_target_pairs={{0,8},{8,16},{16,24},{24,0},{1,9},{9,17},{17,25},{25,1},{2,10},{10... | collective-permute-start | bytes 3145736 | tf_op jit(solution)/shard_map/ppermute | solution.py:42
  114.6 27.7 %copy-start.13 = (f32[1,1024]{1,0:T(1,128)S(1)}, f32[1,1024]{1,0:T(1,128)}, u32[]{:S(2)}) copy-start(f32[1,1024]{1,0:T(1,128)} %get-tuple-element.88) | copy-start | bytes 12292
  114.6 27.7 %copy-start.14 = (f32[1,1024]{1,0:T(1,128)S(1)}, f32[1,1024]{1,0:T(1,128)}, u32[]{:S(2)}) copy-start(f32[1,1024]{1,0:T(1,128)} %get-tuple-element.89) | copy-start | bytes 12292
  114.6 27.7 %copy-start.15 = (f32[1,1024]{1,0:T(1,128)S(1)}, f32[1,1024]{1,0:T(1,128)}, u32[]{:S(2)}) copy-start(f32[1,1024]{1,0:T(1,128)} %get-tuple-element.90) | copy-start | bytes 12292
  142.2 23.4 %copy-start.2 = (f32[1024,32,128]{0,2,1:T(8,128)}, f32[1024,32,128]{0,2,1:T(8,128)S(1)}, u32[]{:S(2)}) copy-start(f32[1024,32,128]{0,2,1:T(8,128)S(1)} %fusion.38) | copy-start | bytes 50331652
  166.5 276.3 %all-reduce.6.cloned.1.call-start = ((), (), s32[]{:S(2)}) async-start(), calls=%async_computation.1 | async-start | bytes 655360 | tf_op jit(solution)/shard_map/psum | solution.py:199
  246.5 6.2 copy-start.1
  289.4 26.1 %collective-permute-start.2 = (f32[1024,2,128]{0,2,1:T(8,128)S(1)}, f32[1024,2,128]{0,2,1:T(8,128)S(1)}, u32[]{:S(2)}, u32[]{:S(2)}) collective-permute-start(f32[1024,2,128]{0,2,1:T(8,128)S(1)} %get-tuple-element.40), channel_id=1, source_target_pairs={{8,0},{16,8},{24,16},{0,24},{9,1},{17,9},{25,17},{1,25},{10,2},{18... | collective-permute-start | bytes 3145736 | tf_op jit(solution)/shard_map/ppermute | solution.py:43
  291.8 71.8 %copy-start.8 = (f32[32,128]{1,0:T(8,128)S(1)}, f32[32,128]{1,0:T(8,128)}, u32[]{:S(2)}) copy-start(f32[32,128]{1,0:T(8,128)} %get-tuple-element.49) | copy-start | bytes 49156
  291.8 71.9 %copy-start.9 = (f32[32,128]{1,0:T(8,128)S(1)}, f32[32,128]{1,0:T(8,128)}, u32[]{:S(2)}) copy-start(f32[32,128]{1,0:T(8,128)} %get-tuple-element.52) | copy-start | bytes 49156
  291.8 71.9 %copy-start.10 = (f32[32,128]{1,0:T(8,128)S(1)}, f32[32,128]{1,0:T(8,128)}, u32[]{:S(2)}) copy-start(f32[32,128]{1,0:T(8,128)} %get-tuple-element.53) | copy-start | bytes 49156
  291.8 71.9 %copy-start.11 = (f32[32,128]{1,0:T(8,128)S(1)}, f32[32,128]{1,0:T(8,128)}, u32[]{:S(2)}) copy-start(f32[32,128]{1,0:T(8,128)} %get-tuple-element.54) | copy-start | bytes 49156
  291.8 71.9 %copy-start.12 = (f32[32,128]{1,0:T(8,128)S(1)}, f32[32,128]{1,0:T(8,128)}, u32[]{:S(2)}) copy-start(f32[32,128]{1,0:T(8,128)} %get-tuple-element.59) | copy-start | bytes 49156
  291.8 44.1 %collective-permute-start.3 = (f32[1024,2,128]{0,2,1:T(8,128)S(1)}, f32[1024,2,128]{0,2,1:T(8,128)S(1)}, u32[]{:S(2)}, u32[]{:S(2)}) collective-permute-start(f32[1024,2,128]{0,2,1:T(8,128)S(1)} %get-tuple-element.41), channel_id=1, source_target_pairs={{0,8},{8,16},{16,24},{24,0},{1,9},{9,17},{17,25},{25,1},{2,10},{10... | collective-permute-start | bytes 3145736 | tf_op jit(solution)/shard_map/ppermute | solution.py:42
  363.6 23.5 %copy-start.4 = (f32[1024,32,128]{0,2,1:T(8,128)}, f32[1024,32,128]{0,2,1:T(8,128)S(1)}, u32[]{:S(2)}) copy-start(f32[1024,32,128]{0,2,1:T(8,128)S(1)} %fusion.22) | copy-start | bytes 50331652
  387.9 275.0 %all-reduce.8.cloned.1.call-start = ((), (), s32[]{:S(2)}) async-start(), calls=%async_computation.2 | async-start | bytes 655360 | tf_op jit(solution)/shard_map/psum | solution.py:199
  509.5 26.1 %collective-permute-start.4 = (f32[1024,2,128]{0,2,1:T(8,128)S(1)}, f32[1024,2,128]{0,2,1:T(8,128)S(1)}, u32[]{:S(2)}, u32[]{:S(2)}) collective-permute-start(f32[1024,2,128]{0,2,1:T(8,128)S(1)} %get-tuple-element.36), channel_id=1, source_target_pairs={{8,0},{16,8},{24,16},{0,24},{9,1},{17,9},{25,17},{1,25},{10,2},{18... | collective-permute-start | bytes 3145736 | tf_op jit(solution)/shard_map/ppermute | solution.py:43
  511.9 71.8 %copy-start.6 = (f32[32,128]{1,0:T(8,128)S(1)}, f32[32,128]{1,0:T(8,128)}, u32[]{:S(2)}) copy-start(f32[32,128]{1,0:T(8,128)} %get-tuple-element.61) | copy-start | bytes 49156
  511.9 71.9 %copy-start.7 = (f32[32,128]{1,0:T(8,128)S(1)}, f32[32,128]{1,0:T(8,128)}, u32[]{:S(2)}) copy-start(f32[32,128]{1,0:T(8,128)} %get-tuple-element.62) | copy-start | bytes 49156
  511.9 44.2 %collective-permute-start.5 = (f32[1024,2,128]{0,2,1:T(8,128)S(1)}, f32[1024,2,128]{0,2,1:T(8,128)S(1)}, u32[]{:S(2)}, u32[]{:S(2)}) collective-permute-start(f32[1024,2,128]{0,2,1:T(8,128)S(1)} %get-tuple-element.37), channel_id=1, source_target_pairs={{0,8},{8,16},{16,24},{24,0},{1,9},{9,17},{17,25},{25,1},{2,10},{10... | collective-permute-start | bytes 3145736 | tf_op jit(solution)/shard_map/ppermute | solution.py:42
  583.7 23.4 %copy-start.3 = (f32[1024,32,128]{0,2,1:T(8,128)}, f32[1024,32,128]{0,2,1:T(8,128)S(1)}, u32[]{:S(2)}) copy-start(f32[1024,32,128]{0,2,1:T(8,128)S(1)} %fusion.6) | copy-start | bytes 50331652
  (1 other events, 6.2 us)
Sparse Core Ops, SparseCore 0:
  166.6 55.9 all-reduce.3
  388.0 54.6 all-reduce.5
  608.1 54.6 all-reduce.7
where the time goes:
time: 724 us; the launch traced here: 713 us
  waiting for transfers between devices  296 us (41%)
  other arithmetic  210 us (29%)
  matrix products  124 us (17%)
  local copies, waits for them, and re-layouts  58.5 us (8%)
  between operations  14.2 us (2%)
  starting transfers between devices  10 us (1%)
    sub x6, other arithmetic, upwind_back(): return center - 0.5 * lam_col * (3.0 * center - 4.0 * nearer + farther)  187 us
    psum x3, waiting for transfers between devices, shards(): summed = lax.psum(raw_moments, 'vel')  165 us
    dot_general x3, matrix products, shards(): jnp.einsum('av,vxy->axy', table, weight * advected, precision=lax.Precisi...  70.1 us
    ppermute x3, waiting for transfers between devices, with_halo(): after = lax.ppermute(first, axis, down)  67.8 us
    ppermute x3, waiting for transfers between devices, with_halo(): before = lax.ppermute(last, axis, up)  63.2 us
    dot_general x3, matrix products, shards(): jnp.einsum('av,axy->vxy', table, coeffs, precision=lax.Precision.HIGHEST)  54.2 us
    unnamed x36, local copies, waits for them, and re-layouts  28.9 us
    unnamed x54, other arithmetic  18.7 us
  transfers between devices with their start and end apart: 9, of which 9 were waited for; matrix products, arithmetic and copies ran while one was open for 0% of the time, Pallas kernels for 0%

commit v1 on v0

--- a/solution.py
+++ b/solution.py
@@ -196,7 +196,7 @@
             "av,vxy->axy", table, weight * advected, precision=lax.Precision.HIGHEST
         )
         zero_cells = jnp.zeros_like(particle_concentration)
-        summed = lax.psum(raw_moments, "vel")
+        summed = jnp.sum(lax.all_gather(raw_moments, "vel"), axis=0)
         polys = hermite_polys(flow_rows, reciprocal_factor)
         coeffs = to_coeffs(to_modes(summed, polys, zero_cells), polys, zero_cells)
         returned = jnp.einsum("av,axy->vxy", table, coeffs, precision=lax.Precision.HIGHEST)

time: 724 us -> 647 us (0.89)
  waiting for transfers between devices: 296 us -> 236 us
  other arithmetic: 210 us -> 197 us
    psum x3 -> x0, waiting for transfers between devices: 165 us -> none  [shards(): summed = lax.psum(raw_moments, 'vel')]
    all_gather x0 -> x3, waiting for transfers between devices: none -> 97.5 us  [shards(): summed = jnp.sum(lax.all_gather(raw_moments, 'vel'), axis=0)]
    unnamed x54, other arithmetic: 18.7 us -> 1.74 us
    unnamed x36 -> x16, local copies, waits for them, and re-layouts: 28.9 us -> 28.9 us
where the time goes in v1:
time: 647 us; the launch traced here: 638 us
  waiting for transfers between devices  236 us (36%)
  other arithmetic  197 us (30%)
  matrix products  124 us (19%)
  local copies, waits for them, and re-layouts  57.5 us (9%)
  between operations  14.2 us (2%)
  starting transfers between devices  9.94 us (2%)
    sub x6, other arithmetic, upwind_back(): return center - 0.5 * lam_col * (3.0 * center - 4.0 * nearer + farther)  187 us
    all_gather x3, waiting for transfers between devices, shards(): summed = jnp.sum(lax.all_gather(raw_moments, 'vel'), axis=0)  97.5 us
    ppermute x3, waiting for transfers between devices, with_halo(): after = lax.ppermute(first, axis, down)  70.5 us
    dot_general x3, matrix products, shards(): jnp.einsum('av,vxy->axy', table, weight * advected, precision=lax.Precisi...  70.1 us
    ppermute x3, waiting for transfers between devices, with_halo(): before = lax.ppermute(last, axis, up)  67.5 us
    dot_general x3, matrix products, shards(): jnp.einsum('av,axy->vxy', table, coeffs, precision=lax.Precision.HIGHEST)  54.2 us
    unnamed x16, local copies, waits for them, and re-layouts  28.9 us
    add x1, local copies, waits for them, and re-layouts, shards(): adjoint = (1.0 - relaxation_rate) * advected + relaxation_rate * returned  17.4 us
  transfers between devices with their start and end apart: 9, of which 9 were waited for; matrix products, arithmetic and copies ran while one was open for 0% of the time, Pallas kernels for 0%

profile of v1, /device:TPU:0, one launch (start us, length us, event | category | flops | bytes accessed | tf_op | source)
XLA Modules:
  0.0 638.0 jit_solution(11818337508419835612)
XLA Ops:
  8.0 16.5 %copy.106 = f32[1024,32,128]{0,2,1:T(8,128)} copy(f32[1024,32,128]{2,1,0:T(8,128)} %param.4) | data formatting | bytes 33554432 | tf_op args[0]
  26.4 34.8 %fusion.46 = f32[1024,32,128]{0,2,1:T(8,128)} fusion(f32[1024,32,128]{0,2,1:T(8,128)} %copy.106, f32[1024,32,2]{0,2,1:T(2,128)S(1)} %get-tuple-element.47, f32[1024,32,2]{0,2,1:T(2,128)S(1)} %get-tuple-element.46, f32[1024]{0:T(1024)S(1)} %bitcast.1800, pred[1024]{0:T(1024)(128)(4,1)S(1)} %get-tuple-element.6), kind=kLoop, calls=%fused_computation.70 | loop fusion | flops 50331648 | bytes 34083840 | tf_op jit(solution)/shard_map/sub | solution.py:151
  68.5 23.6 %collective-permute-done = f32[1024,2,128]{0,2,1:T(8,128)S(1)} collective-permute-done((f32[1024,2,128]{0,2,1:T(8,128)}, f32[1024,2,128]{0,2,1:T(8,128)S(1)}, u32[]{:S(2)}, u32[]{:S(2)}) %collective-permute-start) | collective-permute-done | bytes 1048608 | tf_op jit(solution)/shard_map/ppermute | solution.py:43
  92.1 22.2 %collective-permute-done.1 = f32[1024,2,128]{0,2,1:T(8,128)S(1)} collective-permute-done((f32[1024,2,128]{0,2,1:T(8,128)}, f32[1024,2,128]{0,2,1:T(8,128)S(1)}, u32[]{:S(2)}, u32[]{:S(2)}) %collective-permute-start.1) | collective-permute-done | bytes 1048608 | tf_op jit(solution)/shard_map/ppermute | solution.py:42
  114.3 27.5 %fusion.38 = f32[1024,32,128]{0,2,1:T(8,128)S(1)} fusion(f32[1024,32,128]{0,2,1:T(8,128)} %fusion.46, f32[1024,2,128]{0,2,1:T(8,128)S(1)} %collective-permute-done.1, f32[1024,2,128]{0,2,1:T(8,128)S(1)} %collective-permute-done, f32[1024]{0:T(1024)S(1)} %bitcast.1797, pred[1024]{0:T(1024)(128)(4,1)S(1)} %get-tuple-element.5), kind=kLoop, calls=%fused_computation.62 | loop fusion | flops 50331648 | bytes 35656704 | tf_op jit(solution)/shard_map/sub | solution.py:151
  141.9 23.4 %fusion.86 = f32[20,32,128]{2,0,1:T(8,128)S(1)} fusion(f32[1024,32,128]{0,2,1:T(8,128)S(1)} %fusion.38, f32[32,128]{1,0:T(8,128)S(1)} %get-tuple-element.55, f32[1024]{0:T(1024)S(1)} %bitcast.1809, f32[32,128]{1,0:T(8,128)S(1)} %get-tuple-element.56, f32[1024]{0:T(1024)S(1)} %bitcast.1806, f32[32,128]{1,0:T(8,128)S(1)} %get-tuple-element.58, ...), kind=kOutput, calls=%fused_computation.125 | convolution fusion | flops 1065353216 | bytes 17281024 | tf_op jit(solution)/shard_map/av,vxy->axy/dot_general | solution.py:195
  166.7 33.6 %all-gather.7.cloned.1.call-done = f32[160,32,128]{2,1,0:T(8,128)} async-done(((f32[20,32,128]{2,1,0:T(8,128)}), f32[160,32,128]{2,1,0:T(8,128)}) %all-gather.7.cloned.1.call-update) | async-done | bytes 2621456 | tf_op jit(solution)/shard_map/all_gather | solution.py:199
  203.0 17.5 %multiply_add_fusion.2 = f32[1024,32,128]{0,2,1:T(8,128)S(1)} fusion(f32[1024,32,128]{0,2,1:T(8,128)} %copy-done.3, f32[32,128]{1,0:T(8,128)S(1)} %get-tuple-element.64, f32[32,128]{1,0:T(8,128)S(1)} %get-tuple-element.63, f32[20,32,128]{2,1,0:T(8,128)S(1)} %constant_dynamic-update-slice_fusion, f32[20,1024]{1,0:T(8,128)S(1)} %stack.12), kind=kOutput, calls=%fused_computation.124 | convolution fusion | flops 1019215872 | bytes 33996800 | tf_op jit(solution)/shard_map/av,axy->vxy/dot_general | solution.py:202
  220.6 6.2 copy-done.1
  227.0 34.8 %fusion.30 = f32[1024,32,128]{0,2,1:T(8,128)} fusion(f32[1024,32,128]{0,2,1:T(8,128)} %copy-done.1, f32[1024,32,2]{0,2,1:T(2,128)S(1)} %get-tuple-element.43, f32[1024,32,2]{0,2,1:T(2,128)S(1)} %get-tuple-element.42, f32[1024]{0:T(1024)S(1)} %bitcast.1801, pred[1024]{0:T(1024)(128)(4,1)S(1)} %get-tuple-element.6), kind=kLoop, calls=%fused_computation.54 | loop fusion | flops 50331648 | bytes 34083840 | tf_op jit(solution)/shard_map/sub | solution.py:151
  266.0 23.5 %collective-permute-done.2 = f32[1024,2,128]{0,2,1:T(8,128)S(1)} collective-permute-done((f32[1024,2,128]{0,2,1:T(8,128)S(1)}, f32[1024,2,128]{0,2,1:T(8,128)S(1)}, u32[]{:S(2)}, u32[]{:S(2)}) %collective-permute-start.2) | collective-permute-done | bytes 1048608 | tf_op jit(solution)/shard_map/ppermute | solution.py:43
  289.5 22.6 %collective-permute-done.3 = f32[1024,2,128]{0,2,1:T(8,128)S(1)} collective-permute-done((f32[1024,2,128]{0,2,1:T(8,128)S(1)}, f32[1024,2,128]{0,2,1:T(8,128)S(1)}, u32[]{:S(2)}, u32[]{:S(2)}) %collective-permute-start.3) | collective-permute-done | bytes 1048608 | tf_op jit(solution)/shard_map/ppermute | solution.py:42
  312.1 27.5 %fusion.22 = f32[1024,32,128]{0,2,1:T(8,128)S(1)} fusion(f32[1024,32,128]{0,2,1:T(8,128)} %fusion.30, f32[1024,2,128]{0,2,1:T(8,128)S(1)} %collective-permute-done.3, f32[1024,2,128]{0,2,1:T(8,128)S(1)} %collective-permute-done.2, f32[1024]{0:T(1024)S(1)} %bitcast.1798, pred[1024]{0:T(1024)(128)(4,1)S(1)} %get-tuple-element.5), kind=kLoop, calls=%fused_computation.46 | loop fusion | flops 50331648 | bytes 35656704 | tf_op jit(solution)/shard_map/sub | solution.py:151
  339.7 23.4 %fusion.70 = f32[20,32,128]{2,0,1:T(8,128)S(1)} fusion(f32[1024,32,128]{0,2,1:T(8,128)S(1)} %fusion.22, f32[32,128]{1,0:T(8,128)S(1)} %get-tuple-element.52, f32[32,128]{1,0:T(8,128)S(1)} %get-tuple-element.53, f32[32,128]{1,0:T(8,128)S(1)} %get-tuple-element.59, f32[32,128]{1,0:T(8,128)S(1)} %get-tuple-element.54, f32[32,128]{1,0:T(8,128)S(1)} %get-tuple-element.49, ...), kind=kOutput, calls=%fused_computation.108 | convolution fusion | flops 1065353216 | bytes 17281024 | tf_op jit(solution)/shard_map/av,vxy->axy/dot_general | solution.py:195
  364.2 31.8 %all-gather.9.cloned.1.call-done = f32[160,32,128]{2,1,0:T(8,128)} async-done(((f32[20,32,128]{2,1,0:T(8,128)}), f32[160,32,128]{2,1,0:T(8,128)}) %all-gather.9.cloned.1.call-update) | async-done | bytes 2621456 | tf_op jit(solution)/shard_map/all_gather | solution.py:199
  398.8 17.5 %multiply_add_fusion.1 = f32[1024,32,128]{0,2,1:T(8,128)S(1)} fusion(f32[1024,32,128]{0,2,1:T(8,128)} %copy-done.4, f32[32,128]{1,0:T(8,128)S(1)} %get-tuple-element.66, f32[32,128]{1,0:T(8,128)S(1)} %get-tuple-element.65, f32[20,32,128]{2,1,0:T(8,128)S(1)} %constant_dynamic-update-slice_fusion.20, f32[20,1024]{1,0:T(8,128)S(1)} %stack.12), kind=kOutput, calls=%fused_computation.107 | convolution fusion | flops 1019215872 | bytes 33996800 | tf_op jit(solution)/shard_map/av,axy->vxy/dot_general | solution.py:202
  422.7 34.8 %fusion.14 = f32[1024,32,128]{0,2,1:T(8,128)} fusion(f32[1024,32,128]{0,2,1:T(8,128)} %copy-done, f32[1024,32,2]{0,2,1:T(2,128)S(1)} %get-tuple-element.39, f32[1024,32,2]{0,2,1:T(2,128)S(1)} %get-tuple-element.38, f32[1024]{0:T(1024)S(1)} %bitcast.1802, pred[1024]{0:T(1024)(128)(4,1)S(1)} %get-tuple-element.6), kind=kLoop, calls=%fused_computation.38 | loop fusion | flops 50331648 | bytes 34083840 | tf_op jit(solution)/shard_map/sub | solution.py:151
  461.8 23.4 %collective-permute-done.4 = f32[1024,2,128]{0,2,1:T(8,128)S(1)} collective-permute-done((f32[1024,2,128]{0,2,1:T(8,128)S(1)}, f32[1024,2,128]{0,2,1:T(8,128)S(1)}, u32[]{:S(2)}, u32[]{:S(2)}) %collective-permute-start.4) | collective-permute-done | bytes 1048608 | tf_op jit(solution)/shard_map/ppermute | solution.py:43
  485.2 22.6 %collective-permute-done.5 = f32[1024,2,128]{0,2,1:T(8,128)S(1)} collective-permute-done((f32[1024,2,128]{0,2,1:T(8,128)S(1)}, f32[1024,2,128]{0,2,1:T(8,128)S(1)}, u32[]{:S(2)}, u32[]{:S(2)}) %collective-permute-start.5) | collective-permute-done | bytes 1048608 | tf_op jit(solution)/shard_map/ppermute | solution.py:42
  507.9 27.5 %fusion.6 = f32[1024,32,128]{0,2,1:T(8,128)S(1)} fusion(f32[1024,32,128]{0,2,1:T(8,128)} %fusion.14, f32[1024,2,128]{0,2,1:T(8,128)S(1)} %collective-permute-done.5, f32[1024,2,128]{0,2,1:T(8,128)S(1)} %collective-permute-done.4, f32[1024]{0:T(1024)S(1)} %bitcast.1799, pred[1024]{0:T(1024)(128)(4,1)S(1)} %get-tuple-element.5), kind=kLoop, calls=%fused_computation.30 | loop fusion | flops 50331648 | bytes 35656704 | tf_op jit(solution)/shard_map/sub | solution.py:151
  535.4 23.4 %fusion.54 = f32[20,32,128]{2,0,1:T(8,128)S(1)} fusion(f32[1024,32,128]{0,2,1:T(8,128)S(1)} %fusion.6, f32[32,128]{1,0:T(8,128)S(1)} %get-tuple-element.61, f32[32,128]{1,0:T(8,128)S(1)} %get-tuple-element.62, f32[32,128]{1,0:T(8,128)S(1)} %get-tuple-element.60, f32[32,128]{1,0:T(8,128)S(1)} %get-tuple-element.51, f32[32,128]{1,0:T(8,128)S(1)} %get-tuple-element.48, ...), kind=kOutput, calls=%fused_computation.91 | convolution fusion | flops 1065353216 | bytes 17281024 | tf_op jit(solution)/shard_map/av,vxy->axy/dot_general | solution.py:195
  559.7 32.1 %all-gather.11.cloned.1.call-done = f32[160,32,128]{2,1,0:T(8,128)} async-done(((f32[20,32,128]{2,1,0:T(8,128)}), f32[160,32,128]{2,1,0:T(8,128)}) %all-gather.11.cloned.1.call-update) | async-done | bytes 2621456 | tf_op jit(solution)/shard_map/all_gather | solution.py:199
  594.5 19.1 %multiply_add_fusion = f32[1024,32,128]{0,2,1:T(8,128)} fusion(f32[1024,32,128]{0,2,1:T(8,128)} %copy-done.2, f32[32,128]{1,0:T(8,128)S(1)} %get-tuple-element.15, f32[32,128]{1,0:T(8,128)S(1)} %get-tuple-element.14, f32[20,32,128]{2,1,0:T(8,128)S(1)} %constant_dynamic-update-slice_fusion.40, f32[20,1024]{1,0:T(8,128)S(1)} %stack.12), kind=kOutput, calls=%fused_computation.90 | convolution fusion | flops 1019215872 | bytes 33996800 | tf_op jit(solution)/shard_map/av,axy->vxy/dot_general | solution.py:202
  613.7 17.4 %copy.117 = f32[1024,32,128]{2,1,0:T(8,128)} copy(f32[1024,32,128]{0,2,1:T(8,128)} %multiply_add_fusion) | data formatting | bytes 33554432 | tf_op jit(solution)/shard_map/add | solution.py:203
  (104 shorter events, 37.0 us)
Async XLA Ops:
  6.5 193.7 %all-gather.7.cloned.1.call-start = ((), (), s32[]{:S(2)}) async-start(), calls=%async_computation | async-start | bytes 2949120 | tf_op jit(solution)/shard_map/all_gather | solution.py:199
  26.4 42.1 %copy-start.5 = (f32[3,5,32,128]{3,2,1,0:T(8,128)S(1)}, f32[3,5,32,128]{3,2,1,0:T(8,128)}, u32[]{:S(2)}) copy-start(f32[3,5,32,128]{3,2,1,0:T(8,128)} %param.7) | copy-start | bytes 737284
  64.3 27.8 %collective-permute-start = (f32[1024,2,128]{0,2,1:T(8,128)}, f32[1024,2,128]{0,2,1:T(8,128)S(1)}, u32[]{:S(2)}, u32[]{:S(2)}) collective-permute-start(f32[1024,2,128]{0,2,1:T(8,128)} %get-tuple-element.44), channel_id=1, source_target_pairs={{8,0},{16,8},{24,16},{0,24},{9,1},{17,9},{25,17},{1,25},{10,2},{18... | collective-permute-start | bytes 3145736 | tf_op jit(solution)/shard_map/ppermute | solution.py:43
  68.3 46.1 %collective-permute-start.1 = (f32[1024,2,128]{0,2,1:T(8,128)}, f32[1024,2,128]{0,2,1:T(8,128)S(1)}, u32[]{:S(2)}, u32[]{:S(2)}) collective-permute-start(f32[1024,2,128]{0,2,1:T(8,128)} %get-tuple-element.45), channel_id=1, source_target_pairs={{0,8},{8,16},{16,24},{24,0},{1,9},{9,17},{17,25},{25,1},{2,10},{10... | collective-permute-start | bytes 3145736 | tf_op jit(solution)/shard_map/ppermute | solution.py:42
  141.9 23.4 %copy-start.3 = (f32[1024,32,128]{0,2,1:T(8,128)}, f32[1024,32,128]{0,2,1:T(8,128)S(1)}, u32[]{:S(2)}) copy-start(f32[1024,32,128]{0,2,1:T(8,128)S(1)} %fusion.38) | copy-start | bytes 50331652
  166.1 229.9 %all-gather.9.cloned.1.call-start = ((), (), s32[]{:S(2)}) async-start(), calls=%async_computation.1 | async-start | bytes 2949120 | tf_op jit(solution)/shard_map/all_gather | solution.py:199
  220.6 6.2 copy-start.1
  263.4 26.1 %collective-permute-start.2 = (f32[1024,2,128]{0,2,1:T(8,128)S(1)}, f32[1024,2,128]{0,2,1:T(8,128)S(1)}, u32[]{:S(2)}, u32[]{:S(2)}) collective-permute-start(f32[1024,2,128]{0,2,1:T(8,128)S(1)} %get-tuple-element.40), channel_id=1, source_target_pairs={{8,0},{16,8},{24,16},{0,24},{9,1},{17,9},{25,17},{1,25},{10,2},{18... | collective-permute-start | bytes 3145736 | tf_op jit(solution)/shard_map/ppermute | solution.py:43
  265.9 46.3 %collective-permute-start.3 = (f32[1024,2,128]{0,2,1:T(8,128)S(1)}, f32[1024,2,128]{0,2,1:T(8,128)S(1)}, u32[]{:S(2)}, u32[]{:S(2)}) collective-permute-start(f32[1024,2,128]{0,2,1:T(8,128)S(1)} %get-tuple-element.41), channel_id=1, source_target_pairs={{0,8},{8,16},{16,24},{24,0},{1,9},{9,17},{17,25},{25,1},{2,10},{10... | collective-permute-start | bytes 3145736 | tf_op jit(solution)/shard_map/ppermute | solution.py:42
  339.7 23.4 %copy-start.4 = (f32[1024,32,128]{0,2,1:T(8,128)}, f32[1024,32,128]{0,2,1:T(8,128)S(1)}, u32[]{:S(2)}) copy-start(f32[1024,32,128]{0,2,1:T(8,128)S(1)} %fusion.22) | copy-start | bytes 50331652
  363.9 227.8 %all-gather.11.cloned.1.call-start = ((), (), s32[]{:S(2)}) async-start(), calls=%async_computation.2 | async-start | bytes 2949120 | tf_op jit(solution)/shard_map/all_gather | solution.py:199
  416.3 6.2 copy-start
  459.2 26.1 %collective-permute-start.4 = (f32[1024,2,128]{0,2,1:T(8,128)S(1)}, f32[1024,2,128]{0,2,1:T(8,128)S(1)}, u32[]{:S(2)}, u32[]{:S(2)}) collective-permute-start(f32[1024,2,128]{0,2,1:T(8,128)S(1)} %get-tuple-element.36), channel_id=1, source_target_pairs={{8,0},{16,8},{24,16},{0,24},{9,1},{17,9},{25,17},{1,25},{10,2},{18... | collective-permute-start | bytes 3145736 | tf_op jit(solution)/shard_map/ppermute | solution.py:43
  461.6 46.3 %collective-permute-start.5 = (f32[1024,2,128]{0,2,1:T(8,128)S(1)}, f32[1024,2,128]{0,2,1:T(8,128)S(1)}, u32[]{:S(2)}, u32[]{:S(2)}) collective-permute-start(f32[1024,2,128]{0,2,1:T(8,128)S(1)} %get-tuple-element.37), channel_id=1, source_target_pairs={{0,8},{8,16},{16,24},{24,0},{1,9},{9,17},{17,25},{25,1},{2,10},{10... | collective-permute-start | bytes 3145736 | tf_op jit(solution)/shard_map/ppermute | solution.py:42
  535.4 23.4 %copy-start.2 = (f32[1024,32,128]{0,2,1:T(8,128)}, f32[1024,32,128]{0,2,1:T(8,128)S(1)}, u32[]{:S(2)}) copy-start(f32[1024,32,128]{0,2,1:T(8,128)S(1)} %fusion.6) | copy-start | bytes 50331652
Sparse Core Ops, SparseCore 0:
  166.3 33.9 all-gather.6
  364.1 31.9 all-gather.8
  559.8 31.9 all-gather.10
